TPU v7x, 256 devices: a whole 4x4x8 slice. The times are simulated.
256 devices in a mesh: chan: 64 (over z, x_hi, y), sky: 4 (over x_lo, core).
Axes of the slice: x: 4 (x_hi: 2, x_lo: 2; x = x_hi * 2 + x_lo), y: 4, z: 8, core: 2. Of those that a mesh axis runs over, the one named last changes fastest.
Arguments:
- cube: float32 [512, 1024, 512], P('sky', 'chan'), may hold values from -6 to 6
- shifts: int32 [256], P('chan'), may hold values from -12 to 12
- halfwidth: int32 [256], P('chan'), may hold values from 1 to 4
- taps: float32 [1024, 9], P('chan'), may hold values from 0.1 to 1
- beam_rows: float32 [512, 512], replicated, as said below
- beam_cols: float32 [512, 512], replicated, as said below
Outputs:
- regridded: float32 [512, 1024, 512], P('sky', 'chan')
Inputs may be any that keep to these rules, and one draw needn't show every extreme that they name: beam_rows[i, j] is zero where |i - j| > 8; its diagonal exceeds the sum of the other entries of its row. beam_cols[i, j] is zero where |i - j| > 8; its diagonal exceeds the sum of the other entries of its row.
All inputs are finite; a program needn't handle non-finite values.
Results may differ from a plain program's by a relative error of at most 0.0003.
Values sent between devices are 32-bit elements; how exact they have to be, the bound alone decides.
A program may use at most 64 MiB of HBM per device.

v0:
```python
import jax
import jax.numpy as jnp
from jax import lax
from jax.sharding import PartitionSpec as P

BLK = 4
S_MAX = 12
RADIUS = 4


def with_halo(x, sides, width):
    for axis, dim in sides:
        size, length = (lax.axis_size(axis), x.shape[dim])
        up = [(i, (i + 1) % size) for i in range(size - 1)]
        down = [(j, i) for i, j in up]
        last = lax.slice_in_dim(x, length - width, length, axis=dim)
        first = lax.slice_in_dim(x, 0, width, axis=dim)
        before = lax.ppermute(last, axis, up)
        after = lax.ppermute(first, axis, down)
        x = jnp.concatenate([before, x, after], axis=dim)
    return x


def per_device(cube, shifts, halfwidth, taps, beam_rows, beam_cols):
    local_rows, chans, width = cube.shape
    reach = S_MAX + RADIUS
    taps_count = 2 * RADIUS + 1
    extended = with_halo(cube, (("chan", 1),), reach)
    chan_ids = jnp.arange(chans, dtype=jnp.int32)
    block_ids = chan_ids // BLK
    offsets = jnp.take(shifts, block_ids)
    limits = jnp.take(halfwidth, block_ids)
    tap_ids = jnp.arange(taps_count, dtype=jnp.int32)
    active = jnp.abs(tap_ids - RADIUS)[None, :] <= limits[:, None]
    masked = jnp.where(active, taps, jnp.float32(0.0))
    weights = masked / jnp.sum(masked, axis=1, keepdims=True)
    source = chan_ids[:, None] + reach + offsets[:, None] + tap_ids[None, :] - RADIUS
    positions = jnp.arange(chans + 2 * reach, dtype=jnp.int32)
    band = jnp.sum(
        jnp.where(
            source[:, :, None] == positions[None, None, :], weights[:, :, None], jnp.float32(0.0)
        ),
        axis=1,
    )
    interp = jnp.einsum("ce,hew->hcw", band, extended, precision=lax.Precision.HIGHEST)
    smoothed = jnp.einsum("hcw,vw->hcv", interp, beam_cols, precision=lax.Precision.HIGHEST)
    mixed = jnp.einsum(
        "gh,hcv->gcv",
        beam_rows,
        lax.all_to_all(smoothed, "sky", split_axis=1, concat_axis=0, tiled=True),
        precision=lax.Precision.HIGHEST,
    )
    return lax.all_to_all(mixed, "sky", split_axis=0, concat_axis=1, tiled=True)


def solution(mesh):
    placed = (P("sky", "chan", None), P("chan"), P("chan"), P("chan", None), P(), P())
    return jax.shard_map(
        per_device, mesh=mesh, in_specs=placed, out_specs=P("sky", "chan", None), check_vma=False
    )
```

profile of v0, /device:TPU:124, one launch (start us, length us, event | category | flops | bytes accessed | tf_op | source)
XLA Modules:
  0.0 261.4 jit_solution(18373305950960036583)
XLA Ops:
  0.0 0.0 copy-start
  0.0 4.8 %collective-permute-start = (f32[128,16,512]{2,1,0:T(8,128)}, f32[128,16,512]{2,1,0:T(8,128)}, u32[]{:S(2)}, u32[]{:S(2)}) collective-permute-start(f32[128,16,512]{2,1,0:T(8,128)} %param.8), channel_id=1, source_target_pairs={{0,4},{4,8},{8,12},{12,16},{16,20},{20,24},{24,28},{28,32},{32,36}... | collective-permute-start | bytes 12582920 | tf_op jit(solution)/shard_map/ppermute | solution.py:18
  4.8 1.9 collective-permute-start.1
  6.7 1.3 gather_fusion.1
  8.0 1.3 gather_fusion
  9.4 0.9 fusion.15
  10.3 0.8 fusion.14
  11.0 0.1 copy.15
  11.1 0.1 select_reduce_fusion
  11.3 83.6 %collective-permute-done = f32[128,16,512]{2,1,0:T(8,128)} collective-permute-done((f32[128,16,512]{2,1,0:T(8,128)}, f32[128,16,512]{2,1,0:T(8,128)}, u32[]{:S(2)}, u32[]{:S(2)}) %collective-permute-start) | collective-permute-done | bytes 4194336 | tf_op jit(solution)/shard_map/ppermute | solution.py:18
  94.9 9.8 %collective-permute-done.1 = f32[128,16,512]{2,1,0:T(8,128)} collective-permute-done((f32[128,16,512]{2,1,0:T(8,128)}, f32[128,16,512]{2,1,0:T(8,128)}, u32[]{:S(2)}, u32[]{:S(2)}) %collective-permute-start.1) | collective-permute-done | bytes 4194336 | tf_op jit(solution)/shard_map/ppermute | solution.py:19
  104.7 9.2 %fusion.8 = f32[128,16,512]{2,1,0:T(8,128)S(1)} fusion(f32[128,16,512]{2,1,0:T(8,128)} %collective-permute-done.1, f32[128,16,512]{2,1,0:T(8,128)} %param.8, f32[128,16,512]{2,1,0:T(8,128)} %collective-permute-done, f32[16,48]{1,0:T(8,128)S(1)} %select_reduce_fusion), kind=kOutput, calls=%fused_computation.10 | convolution fusion | flops 610271232 | bytes 16780288 | tf_op jit(solution)/shard_map/ce,hew->hcw/dot_general | solution.py:45
  114.0 0.0 copy-done
  114.0 9.3 %fusion.6 = f32[128,16,512]{2,0,1:T(8,128)S(1)} fusion(f32[128,16,512]{2,1,0:T(8,128)S(1)} %fusion.8, f32[512,512]{1,0:T(8,128)S(1)} %copy-done), kind=kOutput, calls=%fused_computation.8 | convolution fusion | flops 6442450944 | bytes 9437184 | tf_op jit(solution)/shard_map/hcw,vw->hcv/dot_general | solution.py:46
  123.3 51.6 %all_to_all.36 = f32[128,16,512]{2,0,1:T(8,128)} all-to-all(f32[128,16,512]{2,0,1:T(8,128)S(1)} %fusion.6), channel_id=1, replica_groups=mesh['chan'=64,'sky'=4] {'sky'}, dimensions={1} | all-to-all | bytes 8388608 | tf_op jit(solution)/shard_map/all_to_all | solution.py:50
  174.8 5.2 %copy.17 = f32[4,128,4,512]{1,0,3,2:T(4,128)} copy(f32[4,128,4,512]{3,1,2,0:T(8,128)} %bitcast.22) | data formatting | bytes 8388608 | tf_op jit(solution)/shard_map/all_to_all | solution.py:50
  180.1 0.0 copy-start.1
  180.1 5.6 %all_to_all.29 = f32[512,4,512]{0,2,1:T(8,128)} reshape(f32[4,128,4,512]{1,0,3,2:T(4,128)} %copy.17) | data formatting | bytes 8388608 | tf_op jit(solution)/shard_map/all_to_all | solution.py:50
  185.6 0.0 copy-done.1
  185.6 9.9 %convolution_bitcast_fusion = f32[512,4,512]{0,2,1:T(8,128)} fusion(f32[512,4,512]{0,2,1:T(8,128)} %all_to_all.29, f32[512,512]{1,0:T(8,128)S(1)} %copy-done.1), kind=kOutput, calls=%fused_computation.11 | convolution fusion | flops 6442450944 | bytes 9437184 | tf_op jit(solution)/shard_map/gh,hcv->gcv/dot_general | solution.py:47
  195.5 5.4 %copy.18 = f32[512,4,512]{2,1,0:T(4,128)} copy(f32[512,4,512]{0,2,1:T(8,128)} %convolution_bitcast_fusion) | data formatting | bytes 8388608 | tf_op jit(solution)/shard_map/gh,hcv->gcv/dot_general | solution.py:47
  200.9 51.9 %all_to_all.37 = f32[512,4,512]{2,1,0:T(4,128)S(1)} all-to-all(f32[512,4,512]{2,1,0:T(4,128)} %copy.18), channel_id=1, replica_groups=mesh['chan'=64,'sky'=4] {'sky'}, dimensions={0} | all-to-all | bytes 8388608 | tf_op jit(solution)/shard_map/all_to_all | solution.py:53
  252.8 3.3 %copy.19 = f32[128,4,4,512]{3,2,1,0:T(4,128)} copy(f32[128,4,4,512]{3,2,0,1:T(4,128)S(1)} %bitcast.23) | data formatting | bytes 8388608 | tf_op jit(solution)/shard_map/all_to_all | solution.py:53
  256.1 5.3 %all_to_all.33 = f32[128,16,512]{2,1,0:T(8,128)} reshape(f32[128,4,4,512]{3,2,1,0:T(4,128)} %copy.19) | data formatting | bytes 8388608 | tf_op jit(solution)/shard_map/all_to_all | solution.py:53
  (6 shorter events, 0.0 us)
Async XLA Ops:
  0.0 114.0 %copy-start = (f32[512,512]{1,0:T(8,128)S(1)}, f32[512,512]{1,0:T(8,128)}, u32[]{:S(2)}) copy-start(f32[512,512]{1,0:T(8,128)} %param.13) | copy-start | bytes 3145732
  0.0 94.9 %collective-permute-start = (f32[128,16,512]{2,1,0:T(8,128)}, f32[128,16,512]{2,1,0:T(8,128)}, u32[]{:S(2)}, u32[]{:S(2)}) collective-permute-start(f32[128,16,512]{2,1,0:T(8,128)} %param.8), channel_id=1, source_target_pairs={{0,4},{4,8},{8,12},{12,16},{16,20},{20,24},{24,28},{28,32},{32,36}... | collective-permute-start | bytes 12582920 | tf_op jit(solution)/shard_map/ppermute | solution.py:18
  4.8 100.0 %collective-permute-start.1 = (f32[128,16,512]{2,1,0:T(8,128)}, f32[128,16,512]{2,1,0:T(8,128)}, u32[]{:S(2)}, u32[]{:S(2)}) collective-permute-start(f32[128,16,512]{2,1,0:T(8,128)} %param.8), channel_id=1, source_target_pairs={{4,0},{8,4},{12,8},{16,12},{20,16},{24,20},{28,24},{32,28},{36,32}... | collective-permute-start | bytes 12582920 | tf_op jit(solution)/shard_map/ppermute | solution.py:19
  180.1 5.6 %copy-start.1 = (f32[512,512]{1,0:T(8,128)S(1)}, f32[512,512]{1,0:T(8,128)}, u32[]{:S(2)}) copy-start(f32[512,512]{1,0:T(8,128)} %param.12) | copy-start | bytes 3145732
where the time goes:
time: 262 us; the launch traced here: 261 us
  blocking collectives  103 us (39%)
  waiting for transfers between devices  93.5 us (36%)
  matrix products  28.4 us (11%)
  local copies, waits for them, and re-layouts  27.5 us (10%)
  starting transfers between devices  6.68 us (3%)
    ppermute x1, waiting for transfers between devices, with_halo(): before = lax.ppermute(last, axis, up)  83.6 us
    all_to_all x1, blocking collectives, per_device(): return lax.all_to_all(mixed, 'sky', split_axis=0, concat_axis=1, tiled=True)  51.9 us
    all_to_all x1, blocking collectives, per_device(): lax.all_to_all(smoothed, 'sky', split_axis=1, concat_axis=0, tiled=True)  51.6 us
    all_to_all x2, local copies, waits for them, and re-layouts, per_device(): lax.all_to_all(smoothed, 'sky', split_axis=1, concat_axis=0, tiled=True)  10.8 us
    dot_general x1, matrix products, per_device(): jnp.einsum('gh,hcv->gcv', beam_rows, lax.all_to_all(smoothed, 'sky', spli...  9.88 us
    ppermute x1, waiting for transfers between devices, with_halo(): after = lax.ppermute(first, axis, down)  9.84 us
    dot_general x1, matrix products, per_device(): jnp.einsum('hcw,vw->hcv', interp, beam_cols, precision=lax.Precision.HIGH...  9.29 us
    dot_general x1, matrix products, per_device(): jnp.einsum('ce,hew->hcw', band, extended, precision=lax.Precision.HIGHEST)  9.21 us
  transfers between devices with their start and end apart: 2, of which 2 were waited for; matrix products, arithmetic and copies ran while one was open for 2% of the time, Pallas kernels for 0%

commit v1 on v0

--- a/solution.py
+++ b/solution.py
@@ -1,3 +1,4 @@
+import functools
 import jax
 import jax.numpy as jnp
 from jax import lax
@@ -6,6 +7,22 @@
 BLK = 4
 S_MAX = 12
 RADIUS = 4
+
+
+def follow_results_here(slab_in, along_dim, axis_no):
+    next_value = jnp.concatenate(
+        lax.all_to_all(
+            jnp.stack(jnp.split(slab_in, lax.axis_size("sky"), axis=along_dim)),
+            axis_name="sky",
+            split_axis=0,
+            concat_axis=0,
+        ),
+        axis=axis_no,
+    )
+    return next_value
+
+
+watch_point = functools.partial(follow_results_here, along_dim=0, axis_no=1)
 
 
 def with_halo(x, sides, width):
@@ -50,7 +67,7 @@
         lax.all_to_all(smoothed, "sky", split_axis=1, concat_axis=0, tiled=True),
         precision=lax.Precision.HIGHEST,
     )
-    return lax.all_to_all(mixed, "sky", split_axis=0, concat_axis=1, tiled=True)
+    return watch_point(mixed)
 
 
 def solution(mesh):

time: 262 us -> 253 us (0.966)
  local copies, waits for them, and re-layouts: 27.5 us -> 19.4 us
    all_to_all x2 -> x0, local copies, waits for them, and re-layouts: 8.52 us -> none  [per_device(): return lax.all_to_all(mixed, 'sky', split_axis=0, concat_axis=1, tiled=True)]
    reshape x0 -> x1, local copies, waits for them, and re-layouts: none -> 5.45 us  [follow_results_here(): jnp.concatenate(lax.all_to_all(jnp.stack(jnp.split(slab_in, lax.axis_size...]
    dot_general x1 -> x0, local copies, waits for them, and re-layouts: 5.44 us -> none  [per_device(): jnp.einsum('gh,hcv->gcv', beam_rows, lax.all_to_all(smoothed, 'sky', spli...]
where the time goes in v1:
time: 253 us; the launch traced here: 252 us
  blocking collectives  103 us (41%)
  waiting for transfers between devices  93.5 us (37%)
  matrix products  27.1 us (11%)
  local copies, waits for them, and re-layouts  19.4 us (8%)
  starting transfers between devices  6.68 us (3%)
    ppermute x1, waiting for transfers between devices, with_halo(): before = lax.ppermute(last, axis, up)  83.6 us
    all_to_all x1, blocking collectives, per_device(): lax.all_to_all(smoothed, 'sky', split_axis=1, concat_axis=0, tiled=True)  51.6 us
    all_to_all x1, blocking collectives, follow_results_here(): lax.all_to_all(jnp.stack(jnp.split(slab_in, lax.axis_size('sky'), axis=al...  51.6 us
    all_to_all x2, local copies, waits for them, and re-layouts, per_device(): lax.all_to_all(smoothed, 'sky', split_axis=1, concat_axis=0, tiled=True)  10.8 us
    ppermute x1, waiting for transfers between devices, with_halo(): after = lax.ppermute(first, axis, down)  9.84 us
    dot_general x1, matrix products, per_device(): jnp.einsum('hcw,vw->hcv', interp, beam_cols, precision=lax.Precision.HIGH...  9.29 us
    dot_general x1, matrix products, per_device(): jnp.einsum('ce,hew->hcw', band, extended, precision=lax.Precision.HIGHEST)  9.21 us
    dot_general x1, matrix products, per_device(): jnp.einsum('gh,hcv->gcv', beam_rows, lax.all_to_all(smoothed, 'sky', spli...  8.56 us
  transfers between devices with their start and end apart: 2, of which 2 were waited for; matrix products, arithmetic and copies ran while one was open for 2% of the time, Pallas kernels for 0%

profile of v1, /device:TPU:124, one launch (start us, length us, event | category | flops | bytes accessed | tf_op | source)
XLA Modules:
  0.0 252.0 jit_solution(12776664280094749415)
XLA Ops:
  0.0 0.0 copy-start
  0.0 4.8 %collective-permute-start = (f32[128,16,512]{2,1,0:T(8,128)}, f32[128,16,512]{2,1,0:T(8,128)}, u32[]{:S(2)}, u32[]{:S(2)}) collective-permute-start(f32[128,16,512]{2,1,0:T(8,128)} %param.8), channel_id=1, source_target_pairs={{0,4},{4,8},{8,12},{12,16},{16,20},{20,24},{24,28},{28,32},{32,36}... | collective-permute-start | bytes 12582920 | tf_op jit(solution)/shard_map/ppermute | solution.py:35
  4.8 1.9 collective-permute-start.1
  6.7 1.3 gather_fusion.1
  8.0 1.3 gather_fusion
  9.4 0.9 fusion.15
  10.3 0.8 fusion.14
  11.0 0.1 copy.11
  11.1 0.1 select_reduce_fusion
  11.3 83.6 %collective-permute-done = f32[128,16,512]{2,1,0:T(8,128)} collective-permute-done((f32[128,16,512]{2,1,0:T(8,128)}, f32[128,16,512]{2,1,0:T(8,128)}, u32[]{:S(2)}, u32[]{:S(2)}) %collective-permute-start) | collective-permute-done | bytes 4194336 | tf_op jit(solution)/shard_map/ppermute | solution.py:35
  94.9 9.8 %collective-permute-done.1 = f32[128,16,512]{2,1,0:T(8,128)} collective-permute-done((f32[128,16,512]{2,1,0:T(8,128)}, f32[128,16,512]{2,1,0:T(8,128)}, u32[]{:S(2)}, u32[]{:S(2)}) %collective-permute-start.1) | collective-permute-done | bytes 4194336 | tf_op jit(solution)/shard_map/ppermute | solution.py:36
  104.7 9.2 %fusion.8 = f32[128,16,512]{2,1,0:T(8,128)S(1)} fusion(f32[128,16,512]{2,1,0:T(8,128)} %collective-permute-done.1, f32[128,16,512]{2,1,0:T(8,128)} %param.8, f32[128,16,512]{2,1,0:T(8,128)} %collective-permute-done, f32[16,48]{1,0:T(8,128)S(1)} %select_reduce_fusion), kind=kOutput, calls=%fused_computation.11 | convolution fusion | flops 610271232 | bytes 16780288 | tf_op jit(solution)/shard_map/ce,hew->hcw/dot_general | solution.py:62
  114.0 0.0 copy-done
  114.0 9.3 %fusion.6 = f32[128,16,512]{2,0,1:T(8,128)S(1)} fusion(f32[128,16,512]{2,1,0:T(8,128)S(1)} %fusion.8, f32[512,512]{1,0:T(8,128)S(1)} %copy-done), kind=kOutput, calls=%fused_computation.9 | convolution fusion | flops 6442450944 | bytes 9437184 | tf_op jit(solution)/shard_map/hcw,vw->hcv/dot_general | solution.py:63
  123.3 51.6 %all_to_all.23 = f32[128,16,512]{2,0,1:T(8,128)} all-to-all(f32[128,16,512]{2,0,1:T(8,128)S(1)} %fusion.6), channel_id=1, replica_groups=mesh['chan'=64,'sky'=4] {'sky'}, dimensions={1} | all-to-all | bytes 8388608 | tf_op jit(solution)/shard_map/all_to_all | solution.py:67
  174.8 5.2 %copy.13 = f32[4,128,4,512]{1,0,3,2:T(4,128)} copy(f32[4,128,4,512]{3,1,2,0:T(8,128)} %bitcast.30) | data formatting | bytes 8388608 | tf_op jit(solution)/shard_map/all_to_all | solution.py:67
  180.1 0.0 copy-start.1
  180.1 5.6 %all_to_all.19 = f32[512,4,512]{0,2,1:T(8,128)} reshape(f32[4,128,4,512]{1,0,3,2:T(4,128)} %copy.13) | data formatting | bytes 8388608 | tf_op jit(solution)/shard_map/all_to_all | solution.py:67
  185.6 0.0 copy-done.1
  185.6 8.6 %convolution_bitcast_fusion = f32[512,4,512]{0,2,1:T(8,128)S(1)} fusion(f32[512,4,512]{0,2,1:T(8,128)} %all_to_all.19, f32[512,512]{1,0:T(8,128)S(1)} %copy-done.1), kind=kOutput, calls=%fused_computation.12 | convolution fusion | flops 6442450944 | bytes 9437184 | tf_op jit(solution)/shard_map/gh,hcv->gcv/dot_general | solution.py:64
  194.2 0.4 slice_bitcast_fusion.3
  194.6 0.4 pad_maximum_fusion
  195.0 51.6 %all_to_all.24 = f32[4,128,4,512]{1,3,2,0:T(8,128)} all-to-all(f32[4,128,4,512]{1,3,2,0:T(8,128)S(1)} %pad_maximum_fusion), channel_id=1, replica_groups=mesh['chan'=64,'sky'=4] {'sky'}, dimensions={0} | all-to-all | bytes 8388608 | tf_op jit(solution)/shard_map/all_to_all | solution.py:14
  246.6 5.4 %copy.14 = f32[128,16,512]{2,1,0:T(8,128)} copy(f32[128,16,512]{0,2,1:T(8,128)} %bitcast.31) | data formatting | bytes 8388608 | tf_op jit(solution)/shard_map/reshape | solution.py:13
  (6 shorter events, 0.0 us)
Async XLA Ops:
  0.0 114.0 %copy-start = (f32[512,512]{1,0:T(8,128)S(1)}, f32[512,512]{1,0:T(8,128)}, u32[]{:S(2)}) copy-start(f32[512,512]{1,0:T(8,128)} %param.13) | copy-start | bytes 3145732
  0.0 94.9 %collective-permute-start = (f32[128,16,512]{2,1,0:T(8,128)}, f32[128,16,512]{2,1,0:T(8,128)}, u32[]{:S(2)}, u32[]{:S(2)}) collective-permute-start(f32[128,16,512]{2,1,0:T(8,128)} %param.8), channel_id=1, source_target_pairs={{0,4},{4,8},{8,12},{12,16},{16,20},{20,24},{24,28},{28,32},{32,36}... | collective-permute-start | bytes 12582920 | tf_op jit(solution)/shard_map/ppermute | solution.py:35
  4.8 100.0 %collective-permute-start.1 = (f32[128,16,512]{2,1,0:T(8,128)}, f32[128,16,512]{2,1,0:T(8,128)}, u32[]{:S(2)}, u32[]{:S(2)}) collective-permute-start(f32[128,16,512]{2,1,0:T(8,128)} %param.8), channel_id=1, source_target_pairs={{4,0},{8,4},{12,8},{16,12},{20,16},{24,20},{28,24},{32,28},{36,32}... | collective-permute-start | bytes 12582920 | tf_op jit(solution)/shard_map/ppermute | solution.py:36
  180.1 5.6 %copy-start.1 = (f32[512,512]{1,0:T(8,128)S(1)}, f32[512,512]{1,0:T(8,128)}, u32[]{:S(2)}) copy-start(f32[512,512]{1,0:T(8,128)} %param.12) | copy-start | bytes 3145732
